TPU v7x, 128 devices: a whole 4x4x4 slice. The times are simulated.
128 devices in a mesh: blk: 16 (over x_lo, z, core), kv: 8 (over y, x_hi).
Axes of the slice: x: 4 (x_hi: 2, x_lo: 2; x = x_hi * 2 + x_lo), y: 4, z: 4, core: 2. Of those that a mesh axis runs over, the one named last changes fastest.
Arguments:
- hidden: bfloat16 [4096, 2880], P('blk', 'kv'), may hold values from -6 to 6
- gain_attn: float32 [2880], replicated, may hold values from 0.25 to 1.75
- w_q: bfloat16 [2880, 4096], P(None, 'kv'), may hold values from -0.109375 to 0.109375
- w_k: bfloat16 [2880, 512], P(None, 'kv'), may hold values from -0.109375 to 0.109375
- w_v: bfloat16 [2880, 512], P(None, 'kv'), may hold values from -0.109375 to 0.109375
- sinks: float32 [64], P('kv'), may hold values from 3 to 9
- w_o: bfloat16 [4096, 2880], P('kv'), may hold values from -0.75 to 0.75
- gain_moe: float32 [2880], replicated, may hold values from 0.25 to 1.75
- w_router: bfloat16 [2880, 32], replicated, may hold values from -5.1 to 5.1
- w_gate: bfloat16 [32, 2880, 2880], P('blk', None, 'kv'), may hold values from -0.4375 to 0.4375
- w_up: bfloat16 [32, 2880, 2880], P('blk', None, 'kv'), may hold values from -0.4375 to 0.4375
- w_down: bfloat16 [32, 2880, 2880], P('blk', 'kv'), may hold values from -0.013671875 to 0.013671875
- kv_pool: bfloat16 [256, 128, 1024], P('blk', None, 'kv'), may hold values from -160 to 160
- page_table: int32 [16, 16], P('blk'), may hold values from 0 to 255, as said below
- lengths: int32 [16], P('blk'), may hold values from 1 to 2048, as said below
- routes: int32 [4096, 4], P('blk'), may hold values from 0 to 31, all different within a row; in each aligned block of 256 rows (0 to 255, 256 to 511, ...) at most 48 rows name the same one
Outputs:
- mixed: bfloat16 [4096, 2880], P('blk', 'kv')
Inputs may be any that keep to these rules, and one draw needn't show every extreme that they name: `page_table`: row r lists distinct pool pages, except that requests with equal r // 4 share their first pages: the same page numbers, all lying within the cached tokens of every request of the group. A page outside such a shared run belongs to one request only. `lengths`: some request has exactly 2048 cached tokens. `routes`: among the rows of one request no expert is named more than 48 times, a bound that some block reaches.
All inputs are finite; a program needn't handle non-finite values.
Results may differ from a plain program's by a relative error of at most 0.015.
The roundings to bfloat16 on the way count: a program that leaves them out, or rounds other values in their place, can miss the bound.
Values may be sent and summed in bfloat16 or wider, within the bound.
A program may use at most 128 MiB of HBM per device.

v0:
```python
import jax
import jax.numpy as jnp
from jax import lax
from jax.sharding import PartitionSpec as P

HD = 64
EXP_DEV = 2


epsilon = 1e-05
rope_base = 150000.0
clamp_limit = 7.0
glu_alpha = 1.702


def rms_scale(values, gain_vec):
    mean_sq = jnp.mean(values * values, axis=-1, keepdims=True)
    return values * lax.rsqrt(mean_sq + epsilon) * gain_vec


def rotate(vectors, positions):
    half_dim = vectors.shape[-1] // 2
    inv_freq = rope_base ** (-jnp.arange(half_dim, dtype=jnp.float32) / half_dim)
    angles = positions.astype(jnp.float32)[:, None] * inv_freq[None, :]
    cosines = jnp.cos(angles)[:, None, :]
    sines = jnp.sin(angles)[:, None, :]
    front_half = vectors[..., :half_dim]
    back_half = vectors[..., half_dim:]
    return jnp.concatenate(
        [front_half * cosines - back_half * sines, back_half * cosines + front_half * sines],
        axis=-1,
    )


def swiglu(gate_in, up_in):
    gate_in = jnp.minimum(gate_in, clamp_limit)
    up_in = jnp.clip(up_in, -clamp_limit, clamp_limit)
    return (up_in + 1.0) * gate_in * jax.nn.sigmoid(glu_alpha * gate_in)


def attend(normed, length, page_rows, w_q, w_k, w_v, sinks):
    tok_rows = normed.shape[0]
    kv_heads = w_k.shape[1] // HD
    per_group = w_q.shape[1] // w_k.shape[1]
    positions = length + jnp.arange(tok_rows, dtype=jnp.int32)
    queries = jnp.dot(normed, w_q, preferred_element_type=jnp.float32).reshape(
        tok_rows, kv_heads * per_group, HD
    )
    queries = (
        rotate(queries, positions).astype(jnp.bfloat16).reshape(tok_rows, kv_heads, per_group, HD)
    )
    key_new = jnp.dot(normed, w_k, preferred_element_type=jnp.float32).reshape(
        tok_rows, kv_heads, HD
    )
    key_new = rotate(key_new, positions).astype(jnp.bfloat16)
    value_new = (
        jnp.dot(normed, w_v, preferred_element_type=jnp.float32)
        .astype(jnp.bfloat16)
        .reshape(tok_rows, kv_heads, HD)
    )
    cached = page_rows.reshape(-1, kv_heads, 2, HD)
    ctx_len = cached.shape[0]
    key_all = jnp.concatenate([cached[:, :, 0], key_new], axis=0)
    value_all = jnp.concatenate([cached[:, :, 1], value_new], axis=0)
    row_ids = jnp.arange(tok_rows, dtype=jnp.int32)[:, None]
    col_ids = jnp.arange(ctx_len + tok_rows, dtype=jnp.int32)[None, :]
    visible = jnp.where(col_ids < ctx_len, col_ids < length, col_ids - ctx_len <= row_ids)
    scores = jnp.einsum(
        "tgjd,kgd->gjtk", queries, key_all, preferred_element_type=jnp.float32
    ) * HD ** (-0.5)
    scores = jnp.where(visible[None, None], scores, -jnp.inf)
    sink_term = sinks.reshape(kv_heads, per_group)[:, :, None, None]
    row_top = jnp.maximum(jnp.max(scores, axis=-1, keepdims=True), sink_term)
    exp_terms = jnp.exp(scores - row_top)
    denom_sum = jnp.sum(exp_terms, axis=-1, keepdims=True) + jnp.exp(sink_term - row_top)
    weights_attn = (exp_terms / denom_sum).astype(jnp.bfloat16)
    attended = jnp.einsum(
        "gjtk,kgd->tgjd", weights_attn, value_all, preferred_element_type=jnp.float32
    )
    return attended.astype(jnp.bfloat16).reshape(tok_rows, -1)


def expert_slots(route_rows, expert_count):
    expert_ids = route_rows.reshape(-1)
    one_hot = (expert_ids[:, None] == jnp.arange(expert_count, dtype=jnp.int32)[None, :]).astype(
        jnp.int32
    )
    earlier = jnp.cumsum(one_hot, axis=0) - one_hot
    return (expert_ids, jnp.sum(earlier * one_hot, axis=1))


def local(
    hidden,
    gain_attn,
    w_q,
    w_k,
    w_v,
    sinks,
    w_o,
    gain_moe,
    w_router,
    w_gate,
    w_up,
    w_down,
    kv_pool,
    page_table,
    lengths,
    routes,
):
    tok_rows = hidden.shape[0]
    slice_width = hidden.shape[1]
    kv_rank = lax.axis_index("kv")
    full_rows = lax.all_gather(hidden, "kv", axis=1, tiled=True)
    states = full_rows.astype(jnp.float32)
    normed = rms_scale(states, gain_attn).astype(jnp.bfloat16)
    pool_all = lax.all_gather(kv_pool, "blk", axis=0, tiled=True)
    page_rows = jnp.take(pool_all, page_table[0], axis=0)
    page_rows = page_rows.reshape(page_rows.shape[0] * page_rows.shape[1], -1)
    attended = attend(normed, lengths[0], page_rows, w_q, w_k, w_v, sinks)
    partial_value = jnp.dot(attended, w_o, preferred_element_type=jnp.float32)
    shared = lax.psum_scatter(
        partial_value.astype(jnp.bfloat16), "kv", scatter_dimension=1, tiled=True
    ).astype(jnp.float32)
    residual_slice = hidden.astype(jnp.float32) + shared
    total_sq = lax.psum(jnp.sum(residual_slice * residual_slice, axis=1), "kv")
    gain_slice = lax.dynamic_slice_in_dim(gain_moe, kv_rank * slice_width, slice_width, 0)
    scaled = (
        residual_slice
        * lax.rsqrt(total_sq[:, None] / (slice_width * lax.axis_size("kv")) + epsilon)
        * gain_slice
    )
    moe_in = lax.all_gather(scaled.astype(jnp.bfloat16), "kv", axis=1, tiled=True)
    logits = jnp.dot(moe_in, w_router, preferred_element_type=jnp.float32)
    weights = jax.nn.softmax(jnp.take_along_axis(logits, routes, axis=1), axis=1)
    top_count = routes.shape[1]
    blk_count = lax.axis_size("blk")
    experts = EXP_DEV * blk_count
    capacity = max(2, 3 * tok_rows * top_count // (2 * experts))
    expert_ids, slot_ids = expert_slots(routes, experts)
    places = expert_ids * capacity + slot_ids
    outgoing = (
        jnp.zeros((experts * capacity, moe_in.shape[1]), jnp.bfloat16)
        .at[places]
        .set(jnp.repeat(moe_in, top_count, axis=0))
    )
    outgoing = outgoing.reshape(blk_count, EXP_DEV, capacity, -1)
    items = lax.all_to_all(outgoing, "blk", split_axis=0, concat_axis=0, tiled=True)
    gate_val = jnp.einsum("becd,edf->becf", items, w_gate, preferred_element_type=jnp.float32)
    up_val = jnp.einsum("becd,edf->becf", items, w_up, preferred_element_type=jnp.float32)
    act = swiglu(gate_val, up_val).astype(jnp.bfloat16)
    expert_part = jnp.einsum(
        "becf,efd->becd", act, w_down, preferred_element_type=jnp.float32
    ).astype(jnp.bfloat16)
    arrived = lax.all_to_all(expert_part, "blk", split_axis=0, concat_axis=0, tiled=True)
    picked = arrived.reshape(experts * capacity, -1)[places].reshape(tok_rows, top_count, -1)
    terms = jnp.einsum("tk,tkd->td", weights, picked.astype(jnp.float32))
    moe_slice = lax.psum_scatter(
        terms.astype(jnp.bfloat16), "kv", scatter_dimension=1, tiled=True
    ).astype(jnp.float32)
    return (residual_slice + moe_slice).astype(jnp.bfloat16)


def solution(mesh):
    in_specs = (
        P("blk", "kv"),
        P(),
        P(None, "kv"),
        P(None, "kv"),
        P(None, "kv"),
        P("kv"),
        P("kv", None),
        P(),
        P(),
        P("blk", None, "kv"),
        P("blk", None, "kv"),
        P("blk", "kv", None),
        P("blk", None, "kv"),
        P("blk", None),
        P("blk"),
        P("blk", None),
    )
    out_specs = P("blk", "kv")
    return jax.shard_map(local, mesh=mesh, in_specs=in_specs, out_specs=out_specs, check_vma=False)
```

profile of v0, /device:TPU:0, one launch (start us, length us, event | category | flops | bytes accessed | tf_op | source)
XLA Modules:
  0.0 741.4 jit_solution(7495820381546453120)
XLA Ops:
  12.8 48.0 %all-gather.6.cloned.1.call-done = bf16[256,2880]{0,1:T(8,128)(2,1)} async-done(((bf16[256,360]{0,1:T(8,128)(2,1)}), bf16[256,2880]{0,1:T(8,128)(2,1)}) %all-gather.6.cloned.1.call-update) | async-done | bytes 1474576 | tf_op jit(solution)/shard_map/all_gather | solution.py:113
  70.4 43.1 %all-gather.4.cloned.1.call-done = bf16[256,128,128]{2,1,0:T(8,128)(2,1)} async-done(((bf16[16,128,128]{2,1,0:T(8,128)(2,1)}), bf16[256,128,128]{2,1,0:T(8,128)(2,1)}) %all-gather.4.cloned.1.call-update) | async-done | bytes 8388624 | tf_op jit(solution)/shard_map/all_gather | solution.py:116
  113.5 4.8 gather_fusion
  124.5 10.3 %fusion.1 = (f32[8,256]{1,0:T(8,128)S(1)}, f32[2304,256,8]{1,0,2:T(8,128)}) fusion(pred[256,2304]{0,1:T(8,128)(4,1)S(1)} %fusion.16, bf16[256,8,32]{0,2,1:T(8,128)(2,1)} %get-tuple-element.8, bf16[256,8,32]{0,2,1:T(8,128)(2,1)} %get-tuple-element.7, bf16[256,1,32]{0,2,1:T(8,128)(2,1)} %get-tuple-element.12, bf16[256,1,32]{0,2,1:T(8,128)(2,1)} %get-tuple-element.11, ...), kind=kOutput, calls=%fused_computation.8 | convolution fusion | flops 619542528 | bytes 20029440 | tf_op jit(solution)/shard_map/tgjd,kgd->gjtk/dot_general | solution.py:68
  135.4 10.2 %fusion = f32[8,256]{1,0:T(8,128)S(1)} fusion(f32[2304,256,8]{1,0,2:T(8,128)} %get-tuple-element.16, f32[8,256]{1,0:T(8,128)S(1)} %broadcast_maximum_fusion, pred[256,2304]{0,1:T(8,128)(4,1)S(1)} %fusion.16), kind=kLoop, calls=%fused_computation.7 | loop fusion | flops 18872320 | bytes 19480576 | tf_op jit(solution)/shard_map/reduce_sum | solution.py:75
  146.4 9.4 %fusion.30 = bf16[64,8,256]{2,0,1:T(8,128)(2,1)S(1)} fusion(f32[8,256]{1,0:T(8,128)S(1)} %exponential_add_fusion, f32[8,256]{1,0:T(8,128)S(1)} %broadcast_maximum_fusion, f32[2304,256,8]{1,0,2:T(8,128)} %get-tuple-element.16, pred[256,2304]{0,1:T(8,128)(4,1)S(1)} %fusion.16, bf16[256,1,64]{0,2,1:T(8,128)(2,1)} %fusion.37, ...), kind=kOutput, calls=%fused_computation.32 | convolution fusion | flops 628293632 | bytes 20037632 | tf_op jit(solution)/shard_map/gjtk,kgd->tgjd/dot_general | solution.py:77
  158.8 72.6 %reduce-scatter.3.cloned.1.call-done = bf16[256,360]{0,1:T(8,128)(2,1)} async-done(((bf16[256,2880]{0,1:T(8,128)(2,1)}), bf16[256,360]{0,1:T(8,128)(2,1)}) %reduce-scatter.3.cloned.1.call-update) | async-done | bytes 184336 | tf_op jit(solution)/shard_map/reduce_scatter | solution.py:121
  232.4 21.3 %psum.7 = f32[256]{0:T(256)S(1)} all-reduce(f32[256]{0:T(256)S(1)} %multiply_reduce_fusion.1), channel_id=1, replica_groups=mesh['blk'=16,'kv'=8] {'kv'}, use_global_device_ids=true, to_apply=%region_5.6 | all-reduce | flops 256 | bytes 2048 | tf_op jit(solution)/shard_map/psum | solution.py:125
  256.1 9.0 %reduce-window.6 = s32[32,8,128]{2,1,0:T(8,128)S(1)} reduce-window(s32[32,8,128]{2,1,0:T(8,128)S(1)} %fusion.51, s32[]{:T(128)} %constant.26.clone.1), window={size=1x1x128 pad=0_0x0_0x127_0}, to_apply=%region_8.9 | reduce-window | flops 4161536 | bytes 262148 | tf_op jit(solution)/shard_map/reduce-window
  265.6 35.9 %all-gather.8.cloned.1.call-done = bf16[256,2880]{0,1:T(8,128)(2,1)} async-done(((bf16[256,360]{0,1:T(8,128)(2,1)}), bf16[256,2880]{0,1:T(8,128)(2,1)}) %all-gather.8.cloned.1.call-update) | async-done | bytes 1474576 | tf_op jit(solution)/shard_map/all_gather | solution.py:132
  303.4 5.3 broadcast_in_dim.84
  308.7 10.3 %reshape.464 = bf16[1024,2880]{1,0:T(8,128)(2,1)} reshape(bf16[256,4,2880]{2,1,0:T(4,128)(2,1)} %broadcast_in_dim.84) | data formatting | bytes 11796480 | tf_op jit(solution)/shard_map/reshape | solution.py:144
  319.0 15.1 %scatter_custom_fusion = bf16[1536,2880]{1,0:T(8,128)(2,1)} fusion(s32[1024]{0:T(1024)S(1)} %bitcast.123, bf16[1024,2880]{1,0:T(8,128)(2,1)} %reshape.464, bf16[]{:T(256)} %constant.76.clone.1), kind=kCustom, calls=%fused_computation.17 | custom fusion | bytes 8847872 | tf_op jit(solution)/shard_map/scatter | solution.py:144
  334.1 106.9 %all_to_all.10 = bf16[16,2,48,2880]{3,2,1,0:T(8,128)(2,1)S(1)} all-to-all(bf16[16,2,48,2880]{3,2,1,0:T(8,128)(2,1)} %bitcast.118), channel_id=1, replica_groups=mesh['blk'=16,'kv'=8] {'blk'}, dimensions={0} | all-to-all | bytes 17694720 | tf_op jit(solution)/shard_map/all_to_all | solution.py:147
  444.4 7.8 %fusion.4 = f32[2,16,48,360]{3,2,1,0:T(8,128)} fusion(bf16[16,2,48,2880]{3,2,1,0:T(8,128)(2,1)S(1)} %all_to_all.10, bf16[2,2880,360]{1,2,0:T(8,128)(2,1)} %param.25), kind=kOutput, calls=%fused_computation.13 | convolution fusion | flops 3185049600 | bytes 15206400 | tf_op jit(solution)/shard_map/becd,edf->becf/dot_general | solution.py:148
  452.2 16.4 %convert_bitcast_fusion = bf16[16,2,48,2880]{3,2,0,1:T(8,128)(2,1)} fusion(bf16[2,360,2880]{2,1,0:T(8,128)(2,1)} %param.27, f32[2,16,48,360]{3,2,1,0:T(8,128)} %fusion.4, bf16[2,2880,360]{1,2,0:T(8,128)(2,1)} %param.26, bf16[16,2,48,2880]{3,2,1,0:T(8,128)(2,1)} %copy-done.2), kind=kOutput, calls=%fused_computation.12 | convolution fusion | flops 6380052480 | bytes 28200960 | tf_op jit(solution)/shard_map/becf,efd->becd/dot_general | solution.py:151
  468.6 7.7 %copy.68 = bf16[16,2,48,2880]{3,2,1,0:T(8,128)(2,1)} copy(bf16[16,2,48,2880]{3,2,0,1:T(8,128)(2,1)} %convert_bitcast_fusion) | data formatting | bytes 17694720 | tf_op jit(solution)/shard_map/convert_element_type | solution.py:153
  476.3 4.9 all-to-all-start.1
  481.9 8.9 %gather_fusion.2 = f32[1024]{0:T(1024)S(1)} fusion(f32[256,32]{0,1:T(8,128)S(1)} %fusion.76, s32[1024]{0:T(1024)S(1)} %reshape.454), kind=kCustom, calls=%fused_computation.2 | custom fusion | bytes 16384 | tf_op jit(solution)/shard_map/jit(take_along_axis)/gather | solution.py:134
  491.2 122.7 %all-to-all-done.1 = bf16[16,2,48,2880]{3,2,1,0:T(8,128)(2,1)} async-done(((bf16[16,2,48,2880]{3,2,1,0:T(8,128)(2,1)}), bf16[16,2,48,2880]{3,2,1,0:T(8,128)(2,1)}, u32[]{:S(2)}, u32[]{:S(2)}) %all-to-all-start.1) | async-done | bytes 8847392 | tf_op jit(solution)/shard_map/all_to_all | solution.py:154
  613.9 16.4 %gather_fusion.1 = bf16[1024,2880]{1,0:T(8,128)(2,1)} fusion(bf16[1536,2880]{1,0:T(8,128)(2,1)} %bitcast.34, s32[1024]{0:T(1024)S(1)} %broadcast_clamp_fusion), kind=kCustom, calls=%fused_computation.1 | custom fusion | bytes 11800576 | tf_op jit(solution)/shard_map/gather | solution.py:155
  630.3 10.7 %reshape.437 = bf16[256,4,2880]{2,1,0:T(4,128)(2,1)} reshape(bf16[1024,2880]{1,0:T(8,128)(2,1)} %gather_fusion.1) | data formatting | bytes 11796480 | tf_op jit(solution)/shard_map/reshape | solution.py:155
  641.0 11.8 %multiply_reduce_fusion = bf16[256,2880]{1,0:T(8,128)(2,1)} fusion(bf16[256,4,2880]{2,1,0:T(4,128)(2,1)} %reshape.437, f32[256,4]{1,0:T(8,128)S(1)} %copy.78), kind=kLoop, calls=%fused_computation.9 | loop fusion | flops 8110080 | bytes 7376896
  655.4 77.5 %reduce-scatter.5.cloned.1.call-done = bf16[256,360]{0,1:T(8,128)(2,1)} async-done(((bf16[256,2880]{0,1:T(8,128)(2,1)}), bf16[256,360]{0,1:T(8,128)(2,1)}) %reduce-scatter.5.cloned.1.call-update) | async-done | bytes 184336 | tf_op jit(solution)/shard_map/reduce_scatter | solution.py:157
  (97 shorter events, 40.2 us)
Async XLA Ops:
  6.5 149.3 %copy-start = (bf16[512,2880]{0,1:T(8,128)(2,1)S(1)}, bf16[512,2880]{0,1:T(8,128)(2,1)}, u32[]{:S(2)}) copy-start(bf16[512,2880]{0,1:T(8,128)(2,1)} %param.22) | copy-start | bytes 8847364
  6.5 54.3 %all-gather.6.cloned.1.call-start = ((), (), s32[]{:S(2)}) async-start(), calls=%async_computation.5 | async-start | bytes 1658880 | tf_op jit(solution)/shard_map/all_gather | solution.py:113
  7.3 106.2 %all-gather.4.cloned.1.call-start = ((), (), s32[]{:S(2)}) async-start(), calls=%async_computation.4 | async-start | bytes 8912896 | tf_op jit(solution)/shard_map/all_gather | solution.py:116
  8.0 223.4 %reduce-scatter.3.cloned.1.call-start = ((), (), s32[]{:S(2)}) async-start(), calls=%async_computation.6 | async-start | bytes 1658880 | tf_op jit(solution)/shard_map/reduce_scatter | solution.py:121
  60.8 4.8 copy-start.6
  60.8 7.0 copy-start.13
  60.8 7.0 copy-start.14
  65.6 4.0 copy-start.8
  65.6 4.0 copy-start.9
  124.5 10.3 %copy-start.12 = (f32[8]{0:T(128)S(1)}, f32[8]{0:T(128)}, u32[]{:S(2)}) copy-start(f32[8]{0:T(128)} %param.21) | copy-start | bytes 100
  134.8 0.6 copy-start.11
  155.8 75.5 %copy-start.4 = (bf16[256,360]{0,1:T(8,128)(2,1)S(1)}, bf16[256,360]{0,1:T(8,128)(2,1)}, u32[]{:S(2)}) copy-start(bf16[256,360]{0,1:T(8,128)(2,1)} %param.16) | copy-start | bytes 552964
  155.8 99.6 %copy-start.10 = (s32[256,4]{0,1:T(4,128)S(1)}, s32[256,4]{0,1:T(4,128)}, u32[]{:S(2)}) copy-start(s32[256,4]{0,1:T(4,128)} %param.31) | copy-start | bytes 12292
  157.9 143.6 %all-gather.8.cloned.1.call-start = ((), (), s32[]{:S(2)}) async-start(), calls=%async_computation.7 | async-start | bytes 1658880 | tf_op jit(solution)/shard_map/all_gather | solution.py:132
  440.9 3.5 copy-start.2
  476.3 5.2 copy-start.3
  476.3 5.2 copy-start.7
  476.3 137.6 %all-to-all-start.1 = ((bf16[16,2,48,2880]{3,2,1,0:T(8,128)(2,1)}), bf16[16,2,48,2880]{3,2,1,0:T(8,128)(2,1)}, u32[]{:S(2)}, u32[]{:S(2)}) async-start(bf16[16,2,48,2880]{3,2,1,0:T(8,128)(2,1)} %copy.68), calls=%async_computation.2 | async-start | bytes 18087936 | tf_op jit(solution)/shard_map/all_to_all | solution.py:154
  481.2 251.7 %reduce-scatter.5.cloned.1.call-start = ((), (), s32[]{:S(2)}) async-start(), calls=%async_computation.8 | async-start | bytes 1658880 | tf_op jit(solution)/shard_map/reduce_scatter | solution.py:157
  641.0 91.9 %copy-start.5 = (bf16[256,360]{0,1:T(8,128)(2,1)S(1)}, bf16[256,360]{0,1:T(8,128)(2,1)}, u32[]{:S(2)}) copy-start(bf16[256,360]{0,1:T(8,128)(2,1)} %reduce-scatter.3.cloned.1.call-done) | copy-start | bytes 552964
  641.0 93.6 %copy-start.1 = (bf16[512,2880]{0,1:T(8,128)(2,1)S(1)}, bf16[512,2880]{0,1:T(8,128)(2,1)}, u32[]{:S(2)}) copy-start(bf16[512,2880]{0,1:T(8,128)(2,1)} %param.22) | copy-start | bytes 8847364
Sparse Core Ops, SparseCore 0:
  9.6 51.1 all-gather.5
  62.5 50.9 all-gather.3
  158.1 73.2 reduce-scatter.2
  255.5 45.9 all-gather.7
  655.6 77.3 reduce-scatter.4
where the time goes:
time: 751 us; the launch traced here: 741 us
  waiting for transfers between devices  401 us (53%)
  blocking collectives  128 us (17%)
  local copies, waits for them, and re-layouts  95.1 us (13%)
  matrix products  52.3 us (7%)
  other arithmetic  45.2 us (6%)
  between operations  14.3 us (2%)
    all_to_all x1, waiting for transfers between devices, local(): lax.all_to_all(expert_part, 'blk', split_axis=0, concat_axis=0, tiled=True)  123 us
    all_to_all x1, blocking collectives, local(): lax.all_to_all(outgoing, 'blk', split_axis=0, concat_axis=0, tiled=True)  107 us
    reduce_scatter x1, waiting for transfers between devices, local(): lax.psum_scatter(terms.astype(jnp.bfloat16), 'kv', scatter_dimension=1, t...  77.5 us
    reduce_scatter x1, waiting for transfers between devices, local(): lax.psum_scatter(partial_value.astype(jnp.bfloat16), 'kv', scatter_dimens...  72.6 us
    all_gather x1, waiting for transfers between devices, local(): full_rows = lax.all_gather(hidden, 'kv', axis=1, tiled=True)  48 us
    all_gather x1, waiting for transfers between devices, local(): pool_all = lax.all_gather(kv_pool, 'blk', axis=0, tiled=True)  43.1 us
    all_gather x1, waiting for transfers between devices, local(): lax.all_gather(scaled.astype(jnp.bfloat16), 'kv', axis=1, tiled=True)  35.9 us
    psum x1, blocking collectives, local(): total_sq = lax.psum(jnp.sum(residual_slice * residual_slice, axis=1), 'kv')  21.3 us
  transfers between devices with their start and end apart: 6, of which 6 were waited for; matrix products, arithmetic and copies ran while one was open for 5% of the time, Pallas kernels for 0%

commit v1 on v0

--- a/solution.py
+++ b/solution.py
@@ -87,6 +87,20 @@
     )
     earlier = jnp.cumsum(one_hot, axis=0) - one_hot
     return (expert_ids, jnp.sum(earlier * one_hot, axis=1))
+
+
+def gather_kv(block):
+    count = lax.axis_size("kv")
+    rows, width = block.shape
+    spread = jnp.broadcast_to(block[:, None, :], (rows, count, width))
+    return lax.all_to_all(spread, "kv", 1, 1, tiled=True).reshape(rows, count * width)
+
+
+def reduce_kv(block):
+    count = lax.axis_size("kv")
+    rows, width = block.shape
+    parts = lax.all_to_all(block.reshape(rows, count, width // count), "kv", 1, 1, tiled=True)
+    return jnp.sum(parts.astype(jnp.float32), axis=1)
 
 
 def local(
@@ -110,7 +124,7 @@
     tok_rows = hidden.shape[0]
     slice_width = hidden.shape[1]
     kv_rank = lax.axis_index("kv")
-    full_rows = lax.all_gather(hidden, "kv", axis=1, tiled=True)
+    full_rows = gather_kv(hidden)
     states = full_rows.astype(jnp.float32)
     normed = rms_scale(states, gain_attn).astype(jnp.bfloat16)
     pool_all = lax.all_gather(kv_pool, "blk", axis=0, tiled=True)
@@ -118,45 +132,50 @@
     page_rows = page_rows.reshape(page_rows.shape[0] * page_rows.shape[1], -1)
     attended = attend(normed, lengths[0], page_rows, w_q, w_k, w_v, sinks)
     partial_value = jnp.dot(attended, w_o, preferred_element_type=jnp.float32)
-    shared = lax.psum_scatter(
-        partial_value.astype(jnp.bfloat16), "kv", scatter_dimension=1, tiled=True
-    ).astype(jnp.float32)
+    shared = reduce_kv(partial_value.astype(jnp.bfloat16))
     residual_slice = hidden.astype(jnp.float32) + shared
     total_sq = lax.psum(jnp.sum(residual_slice * residual_slice, axis=1), "kv")
     gain_slice = lax.dynamic_slice_in_dim(gain_moe, kv_rank * slice_width, slice_width, 0)
-    scaled = (
+    moe_slice_in = (
         residual_slice
         * lax.rsqrt(total_sq[:, None] / (slice_width * lax.axis_size("kv")) + epsilon)
         * gain_slice
-    )
-    moe_in = lax.all_gather(scaled.astype(jnp.bfloat16), "kv", axis=1, tiled=True)
-    logits = jnp.dot(moe_in, w_router, preferred_element_type=jnp.float32)
+    ).astype(jnp.bfloat16)
+    router_rows = lax.dynamic_slice_in_dim(w_router, kv_rank * slice_width, slice_width, 0)
+    logits = lax.psum(
+        jnp.dot(moe_slice_in, router_rows, preferred_element_type=jnp.float32), "kv"
+    )
     weights = jax.nn.softmax(jnp.take_along_axis(logits, routes, axis=1), axis=1)
     top_count = routes.shape[1]
     blk_count = lax.axis_size("blk")
     experts = EXP_DEV * blk_count
     capacity = max(2, 3 * tok_rows * top_count // (2 * experts))
     expert_ids, slot_ids = expert_slots(routes, experts)
-    places = expert_ids * capacity + slot_ids
-    outgoing = (
-        jnp.zeros((experts * capacity, moe_in.shape[1]), jnp.bfloat16)
-        .at[places]
-        .set(jnp.repeat(moe_in, top_count, axis=0))
-    )
-    outgoing = outgoing.reshape(blk_count, EXP_DEV, capacity, -1)
-    items = lax.all_to_all(outgoing, "blk", split_axis=0, concat_axis=0, tiled=True)
+    places = (expert_ids * capacity + slot_ids).reshape(tok_rows, top_count)
+    slot_index = jnp.arange(experts * capacity, dtype=jnp.int32)
+    picks = places[:, :, None] == slot_index[None, None, :]
+    dispatch = jnp.any(picks, axis=1).astype(jnp.bfloat16)
+    outgoing = jnp.dot(dispatch.T, moe_slice_in, preferred_element_type=jnp.float32).astype(
+        jnp.bfloat16
+    )
+    outgoing = outgoing.reshape(blk_count, EXP_DEV * capacity, slice_width)
+    items = lax.all_to_all(outgoing, "blk", 0, 0, tiled=True)
+    items = gather_kv(items.reshape(blk_count * EXP_DEV * capacity, slice_width))
+    items = items.reshape(blk_count, EXP_DEV, capacity, -1)
     gate_val = jnp.einsum("becd,edf->becf", items, w_gate, preferred_element_type=jnp.float32)
     up_val = jnp.einsum("becd,edf->becf", items, w_up, preferred_element_type=jnp.float32)
     act = swiglu(gate_val, up_val).astype(jnp.bfloat16)
     expert_part = jnp.einsum(
         "becf,efd->becd", act, w_down, preferred_element_type=jnp.float32
     ).astype(jnp.bfloat16)
-    arrived = lax.all_to_all(expert_part, "blk", split_axis=0, concat_axis=0, tiled=True)
-    picked = arrived.reshape(experts * capacity, -1)[places].reshape(tok_rows, top_count, -1)
-    terms = jnp.einsum("tk,tkd->td", weights, picked.astype(jnp.float32))
-    moe_slice = lax.psum_scatter(
-        terms.astype(jnp.bfloat16), "kv", scatter_dimension=1, tiled=True
-    ).astype(jnp.float32)
+    expert_out = reduce_kv(expert_part.reshape(blk_count * EXP_DEV * capacity, -1))
+    expert_out = expert_out.astype(jnp.bfloat16).reshape(blk_count, EXP_DEV * capacity, slice_width)
+    arrived = lax.all_to_all(expert_out, "blk", 0, 0, tiled=True)
+    arrived = arrived.reshape(experts * capacity, slice_width)
+    picked = jnp.einsum(
+        "tkp,pd->tkd", picks.astype(jnp.bfloat16), arrived, preferred_element_type=jnp.float32
+    )
+    moe_slice = jnp.einsum("tk,tkd->td", weights, picked)
     return (residual_slice + moe_slice).astype(jnp.bfloat16)
 
 

time: 751 us -> 591 us (0.79)
  waiting for transfers between devices: 401 us -> 46.9 us
  blocking collectives: 128 us -> 301 us
  starting transfers between devices: 5.05 us -> 19.1 us
    reduce_scatter x2 -> x0, waiting for transfers between devices: 150 us -> none  [the longest x1 77.5 us: local(): lax.psum_scatter(terms.astype(jnp.bfloat16), 'kv', scatter_dimension=1, t...]
    all_to_all x1 -> x3, blocking collectives: 107 us -> 234 us  [the longest x1 106 us: reduce_kv(): lax.all_to_all(block.reshape(rows, count, width // count), 'kv', 1, 1, ti...]
    all_to_all x1 -> x3, waiting for transfers between devices: 123 us -> 33.3 us  [the longest x1 23.3 us: gather_kv(): lax.all_to_all(spread, 'kv', 1, 1, tiled=True).reshape(rows, count * width)]
    all_gather x2 -> x0, waiting for transfers between devices: 83.9 us -> none  [the longest x1 48 us: local(): full_rows = lax.all_gather(hidden, 'kv', axis=1, tiled=True)]
    another operation x2 -> x5, local copies, waits for them, and re-layouts: 0.08 us -> 48.7 us  [the longest x2 32.2 us: reduce_kv(): block.reshape(rows, count, width // count)]
    psum x0 -> x1, blocking collectives: none -> 46.8 us  [local(): lax.psum(jnp.dot(moe_slice_in, router_rows, preferred_element_type=jnp.fl...]
    all_gather x1, waiting for transfers between devices: 43.1 us -> 12.8 us  [local(): pool_all = lax.all_gather(kv_pool, 'blk', axis=0, tiled=True)]
    reshape x2 -> x0, local copies, waits for them, and re-layouts: 21 us -> none  [the longest x1 10.7 us: local(): arrived.reshape(experts * capacity, -1)[places]]
  transfers between devices with their start and end apart: 6 -> 4, of which waited for: 6 -> 3; matrix products, arithmetic and copies ran while one was open for 5% -> 8% of each run, Pallas kernels for 0% -> 0%
where the time goes in v1:
time: 591 us; the launch traced here: 579 us
  blocking collectives  301 us (51%)
  local copies, waits for them, and re-layouts  102 us (17%)
  matrix products  53.5 us (9%)
  waiting for transfers between devices  46.9 us (8%)
  other arithmetic  41.9 us (7%)
  starting transfers between devices  19.1 us (3%)
  between operations  14.7 us (2%)
    all_to_all x1, blocking collectives, reduce_kv(): lax.all_to_all(block.reshape(rows, count, width // count), 'kv', 1, 1, ti...  106 us
    all_to_all x1, blocking collectives, gather_kv(): lax.all_to_all(spread, 'kv', 1, 1, tiled=True).reshape(rows, count * width)  105 us
    psum x1, blocking collectives, local(): lax.psum(jnp.dot(moe_slice_in, router_rows, preferred_element_type=jnp.fl...  46.8 us
    another operation x2, local copies, waits for them, and re-layouts, reduce_kv(): block.reshape(rows, count, width // count)  32.2 us
    all_to_all x1, waiting for transfers between devices, gather_kv(): lax.all_to_all(spread, 'kv', 1, 1, tiled=True).reshape(rows, count * width)  23.3 us
    all_to_all x1, blocking collectives, local(): items = lax.all_to_all(outgoing, 'blk', 0, 0, tiled=True)  23.2 us
    psum x1, blocking collectives, local(): total_sq = lax.psum(jnp.sum(residual_slice * residual_slice, axis=1), 'kv')  20.5 us
    another operation x1, local copies, waits for them, and re-layouts, local(): items = items.reshape(blk_count, EXP_DEV, capacity, -1)  16.4 us
  transfers between devices with their start and end apart: 4, of which 3 were waited for; matrix products, arithmetic and copies ran while one was open for 8% of the time, Pallas kernels for 0%

profile of v1, /device:TPU:0, one launch (start us, length us, event | category | flops | bytes accessed | tf_op | source)
XLA Modules:
  0.0 579.4 jit_solution(307813837527939568)
XLA Ops:
  9.5 7.0 %all-to-all-start = ((bf16[256,8,360]{0,2,1:T(8,128)(2,1)}), bf16[256,8,360]{0,2,1:T(8,128)(2,1)}, u32[]{:S(2)}, u32[]{:S(2)}) async-start(bf16[256,8,360]{0,2,1:T(8,128)(2,1)} %broadcast_in_dim.84), calls=%async_computation | async-start | bytes 2949120 | tf_op jit(solution)/shard_map/all_to_all | solution.py:96
  28.6 23.3 %all-to-all-done = bf16[256,8,360]{0,2,1:T(8,128)(2,1)} async-done(((bf16[256,8,360]{0,2,1:T(8,128)(2,1)}), bf16[256,8,360]{0,2,1:T(8,128)(2,1)}, u32[]{:S(2)}, u32[]{:S(2)}) %all-to-all-start) | async-done | bytes 1474592 | tf_op jit(solution)/shard_map/all_to_all | solution.py:96
  61.7 12.8 %all-gather.2.cloned.1.call-done = bf16[256,128,128]{2,1,0:T(8,128)(2,1)} async-done(((bf16[16,128,128]{2,1,0:T(8,128)(2,1)}), bf16[256,128,128]{2,1,0:T(8,128)(2,1)}) %all-gather.2.cloned.1.call-update) | async-done | bytes 8388624 | tf_op jit(solution)/shard_map/all_gather | solution.py:130
  74.5 5.0 gather_fusion
  85.6 10.3 %fusion.1 = (f32[8,256]{1,0:T(8,128)S(1)}, f32[2304,256,8]{1,0,2:T(8,128)}) fusion(pred[256,2304]{0,1:T(8,128)(4,1)S(1)} %fusion.16, bf16[256,8,32]{0,2,1:T(8,128)(2,1)} %get-tuple-element.8, bf16[256,8,32]{0,2,1:T(8,128)(2,1)} %get-tuple-element.7, bf16[256,1,32]{0,2,1:T(8,128)(2,1)} %get-tuple-element.12, bf16[256,1,32]{0,2,1:T(8,128)(2,1)} %get-tuple-element.11, ...), kind=kOutput, calls=%fused_computation.6 | convolution fusion | flops 619542528 | bytes 20029440 | tf_op jit(solution)/shard_map/tgjd,kgd->gjtk/dot_general | solution.py:68
  96.5 10.2 %fusion = f32[8,256]{1,0:T(8,128)S(1)} fusion(f32[2304,256,8]{1,0,2:T(8,128)} %get-tuple-element.16, f32[8,256]{1,0:T(8,128)S(1)} %broadcast_maximum_fusion, pred[256,2304]{0,1:T(8,128)(4,1)S(1)} %fusion.16), kind=kLoop, calls=%fused_computation.5 | loop fusion | flops 18872320 | bytes 19480576 | tf_op jit(solution)/shard_map/reduce_sum | solution.py:75
  107.6 9.4 %fusion.30 = bf16[64,8,256]{2,0,1:T(8,128)(2,1)S(1)} fusion(f32[8,256]{1,0:T(8,128)S(1)} %exponential_add_fusion, f32[8,256]{1,0:T(8,128)S(1)} %broadcast_maximum_fusion, f32[2304,256,8]{1,0,2:T(8,128)} %get-tuple-element.16, pred[256,2304]{0,1:T(8,128)(4,1)S(1)} %fusion.16, bf16[256,1,64]{0,2,1:T(8,128)(2,1)} %fusion.37, ...), kind=kOutput, calls=%fused_computation.34 | convolution fusion | flops 628293632 | bytes 20037632 | tf_op jit(solution)/shard_map/gjtk,kgd->tgjd/dot_general | solution.py:77
  119.0 7.7 %all-to-all-start.1 = ((bf16[256,8,360]{0,2,1:T(8,128)(2,1)}), bf16[256,8,360]{0,2,1:T(8,128)(2,1)S(1)}, u32[]{:S(2)}, u32[]{:S(2)}) async-start(bf16[256,8,360]{0,2,1:T(8,128)(2,1)} %bitcast.141), calls=%async_computation.1 | async-start | bytes 2949120 | tf_op jit(solution)/shard_map/all_to_all | solution.py:102
  127.1 9.0 %reduce-window.6 = s32[32,8,128]{2,1,0:T(8,128)S(1)} reduce-window(s32[32,8,128]{2,1,0:T(8,128)S(1)} %fusion.51, s32[]{:T(128)} %constant.26.clone.1), window={size=1x1x128 pad=0_0x0_0x127_0}, to_apply=%region_9.10 | reduce-window | flops 4161536 | bytes 262148 | tf_op jit(solution)/shard_map/reduce-window
  138.8 10.1 %all-to-all-done.1 = bf16[256,8,360]{0,2,1:T(8,128)(2,1)S(1)} async-done(((bf16[256,8,360]{0,2,1:T(8,128)(2,1)}), bf16[256,8,360]{0,2,1:T(8,128)(2,1)S(1)}, u32[]{:S(2)}, u32[]{:S(2)}) %all-to-all-start.1) | async-done | bytes 1474592 | tf_op jit(solution)/shard_map/all_to_all | solution.py:102
  149.2 20.5 %psum.14 = f32[256]{0:T(256)S(1)} all-reduce(f32[256]{0:T(256)S(1)} %multiply_reduce_fusion.2), channel_id=1, replica_groups=mesh['blk'=16,'kv'=8] {'kv'}, use_global_device_ids=true, to_apply=%region_5.6 | all-reduce | flops 256 | bytes 2048 | tf_op jit(solution)/shard_map/psum | solution.py:137
  171.0 23.2 %all_to_all.30 = bf16[16,96,360]{2,1,0:T(8,128)(2,1)S(1)} all-to-all(bf16[16,96,360]{2,1,0:T(8,128)(2,1)S(1)} %bitcast.138), channel_id=1, replica_groups=mesh['blk'=16,'kv'=8] {'blk'}, dimensions={0} | all-to-all | bytes 2211840 | tf_op jit(solution)/shard_map/all_to_all | solution.py:162
  195.4 104.7 %all_to_all.31 = bf16[1536,8,360]{0,2,1:T(8,128)(2,1)} all-to-all(bf16[1536,8,360]{0,2,1:T(8,128)(2,1)S(1)} %broadcast_in_dim.91), channel_id=1, replica_groups=mesh['blk'=16,'kv'=8] {'kv'}, dimensions={1} | all-to-all | bytes 17694720 | tf_op jit(solution)/shard_map/all_to_all | solution.py:96
  300.1 12.7 %copy.120 = bf16[1536,8,360]{2,1,0:T(8,128)(2,1)} copy(bf16[1536,8,360]{0,2,1:T(8,128)(2,1)} %all_to_all.31) | data formatting | bytes 17694720 | tf_op jit(solution)/shard_map/all_to_all | solution.py:96
  312.8 16.4 %reshape_reshape.7 = bf16[16,2,48,2880]{3,2,1,0:T(8,128)(2,1)} reshape(bf16[1536,8,360]{2,1,0:T(8,128)(2,1)} %copy.120) | data formatting | bytes 17694720 | tf_op jit(solution)/shard_map/reshape;reshape | solution.py:164
  329.2 8.8 %fusion.4 = f32[2,16,48,360]{3,2,1,0:T(8,128)S(1)} fusion(bf16[16,2,48,2880]{3,2,1,0:T(8,128)(2,1)} %reshape_reshape.7, bf16[2,2880,360]{1,2,0:T(8,128)(2,1)} %param.25), kind=kOutput, calls=%fused_computation.10 | convolution fusion | flops 3185049600 | bytes 15206400 | tf_op jit(solution)/shard_map/becd,edf->becf/dot_general | solution.py:165
  338.0 16.1 %convert_bitcast_fusion = bf16[16,2,48,2880]{3,2,0,1:T(8,128)(2,1)} fusion(bf16[2,360,2880]{2,1,0:T(8,128)(2,1)} %param.27, f32[2,16,48,360]{3,2,1,0:T(8,128)S(1)} %fusion.4, bf16[2,2880,360]{1,2,0:T(8,128)(2,1)} %param.26, bf16[16,2,48,2880]{3,2,1,0:T(8,128)(2,1)} %reshape_reshape.7), kind=kOutput, calls=%fused_computation.9 | convolution fusion | flops 6380052480 | bytes 28200960 | tf_op jit(solution)/shard_map/becf,efd->becd/dot_general | solution.py:168
  354.1 7.7 %copy.123 = bf16[16,2,48,2880]{3,2,1,0:T(8,128)(2,1)} copy(bf16[16,2,48,2880]{3,2,0,1:T(8,128)(2,1)} %convert_bitcast_fusion) | data formatting | bytes 17694720 | tf_op jit(solution)/shard_map/convert_element_type | solution.py:170
  361.8 19.5 %reshape_reshape.8 = bf16[1536,8,360]{2,1,0:T(8,128)(2,1)} reshape(bf16[16,2,48,2880]{3,2,1,0:T(8,128)(2,1)} %copy.123) | data formatting | bytes 17694720 | tf_op jit(solution)/shard_map/reshape;reshape | solution.py:102
  381.3 12.8 %copy.124 = bf16[1536,8,360]{0,2,1:T(8,128)(2,1)} copy(bf16[1536,8,360]{2,1,0:T(8,128)(2,1)} %reshape_reshape.8) | data formatting | bytes 17694720 | tf_op jit(solution)/shard_map/reshape;reshape | solution.py:102
  394.0 106.3 %all_to_all.32 = bf16[1536,8,360]{0,2,1:T(8,128)(2,1)} all-to-all(bf16[1536,8,360]{0,2,1:T(8,128)(2,1)} %copy.124), channel_id=1, replica_groups=mesh['blk'=16,'kv'=8] {'kv'}, dimensions={1} | all-to-all | bytes 17694720 | tf_op jit(solution)/shard_map/all_to_all | solution.py:102
  500.3 5.4 reduce_sum.75
  512.8 46.8 %psum.15 = f32[256,32]{0,1:T(8,128)S(1)} all-reduce(f32[256,32]{0,1:T(8,128)S(1)} %fusion.60), channel_id=1, replica_groups=mesh['blk'=16,'kv'=8] {'kv'}, use_global_device_ids=true, to_apply=%region_6.7 | all-reduce | flops 8192 | bytes 65536 | tf_op jit(solution)/shard_map/psum | solution.py:145
  559.5 8.6 %gather_fusion.1 = f32[1024]{0:T(1024)S(1)} fusion(f32[256,32]{0,1:T(8,128)S(1)} %psum.15, s32[1024]{0:T(1024)S(1)} %reshape.438), kind=kCustom, calls=%fused_computation.1 | custom fusion | bytes 16384 | tf_op jit(solution)/shard_map/jit(take_along_axis)/gather | solution.py:148
  (107 shorter events, 50.6 us)
Async XLA Ops:
  6.5 110.4 %copy-start = (bf16[512,2880]{0,1:T(8,128)(2,1)S(1)}, bf16[512,2880]{0,1:T(8,128)(2,1)}, u32[]{:S(2)}) copy-start(bf16[512,2880]{0,1:T(8,128)(2,1)} %param.22) | copy-start | bytes 8847364
  6.5 10.7 %copy-start.18 = (s32[1,16]{1,0:T(1,128)S(1)}, s32[1,16]{1,0:T(1,128)}, u32[]{:S(2)}) copy-start(s32[1,16]{1,0:T(1,128)} %param.29) | copy-start | bytes 196
  6.5 11.9 %copy-start.9 = (f32[2880]{0:T(1024)S(1)}, f32[2880]{0:T(1024)}, u32[]{:S(2)}) copy-start(f32[2880]{0:T(1024)} %param.17) | copy-start | bytes 34564
  6.5 68.0 %all-gather.2.cloned.1.call-start = ((), (), s32[]{:S(2)}) async-start(), calls=%async_computation.6 | async-start | bytes 8912896 | tf_op jit(solution)/shard_map/all_gather | solution.py:130
  9.5 42.4 %all-to-all-start = ((bf16[256,8,360]{0,2,1:T(8,128)(2,1)}), bf16[256,8,360]{0,2,1:T(8,128)(2,1)}, u32[]{:S(2)}, u32[]{:S(2)}) async-start(bf16[256,8,360]{0,2,1:T(8,128)(2,1)} %broadcast_in_dim.84), calls=%async_computation | async-start | bytes 2949120 | tf_op jit(solution)/shard_map/all_to_all | solution.py:96
  17.2 7.2 %copy-start.13 = (f32[256]{0:T(256)}, f32[256]{0:T(256)S(1)}, u32[]{:S(2)}) copy-start(f32[256]{0:T(256)S(1)} %add_convert_fusion.2) | copy-start | bytes 3076
  18.5 6.0 %copy-start.15 = (f32[32]{0:T(128)}, f32[32]{0:T(128)S(1)}, u32[]{:S(2)}) copy-start(f32[32]{0:T(128)S(1)} %multiply_power_fusion) | copy-start | bytes 388
  51.9 3.8 copy-start.4
  51.9 4.8 copy-start.5
  53.8 3.3 copy-start.14
  53.8 3.3 copy-start.16
  53.8 4.1 copy-start.10
  56.7 3.2 copy-start.2
  59.8 1.0 copy-start.6
  59.8 1.0 copy-start.7
  60.9 22.9 %copy-start.12 = (pred[2048]{0:T(1024)(128)(4,1)S(1)}, pred[2048]{0:T(1024)(128)(4,1)}, u32[]{:S(2)}) copy-start(pred[2048]{0:T(1024)(128)(4,1)} %broadcast_bitcast_fusion) | copy-start | bytes 6148
  85.6 10.3 %copy-start.17 = (f32[8]{0:T(128)S(1)}, f32[8]{0:T(128)}, u32[]{:S(2)}) copy-start(f32[8]{0:T(128)} %param.21) | copy-start | bytes 100
  95.9 0.6 copy-start.11
  119.0 7.7 %copy-start.8 = (s32[256,4]{0,1:T(4,128)S(1)}, s32[256,4]{0,1:T(4,128)}, u32[]{:S(2)}) copy-start(s32[256,4]{0,1:T(4,128)} %param.31) | copy-start | bytes 12292
  119.0 30.1 %copy-start.3 = (bf16[256,360]{0,1:T(8,128)(2,1)S(1)}, bf16[256,360]{0,1:T(8,128)(2,1)}, u32[]{:S(2)}) copy-start(bf16[256,360]{0,1:T(8,128)(2,1)} %param.16) | copy-start | bytes 552964
  119.0 29.9 %all-to-all-start.1 = ((bf16[256,8,360]{0,2,1:T(8,128)(2,1)}), bf16[256,8,360]{0,2,1:T(8,128)(2,1)S(1)}, u32[]{:S(2)}, u32[]{:S(2)}) async-start(bf16[256,8,360]{0,2,1:T(8,128)(2,1)} %bitcast.141), calls=%async_computation.1 | async-start | bytes 2949120 | tf_op jit(solution)/shard_map/all_to_all | solution.py:102
  507.1 61.3 %all-to-all-start.5 = ((bf16[16,96,360]{2,1,0:T(8,128)(2,1)}), bf16[16,96,360]{2,1,0:T(8,128)(2,1)}, u32[]{:S(2)}, u32[]{:S(2)}) async-start(bf16[16,96,360]{2,1,0:T(8,128)(2,1)} %bitcast.38), calls=%async_computation.5 | async-start | bytes 2359296 | tf_op jit(solution)/shard_map/all_to_all | solution.py:173
  568.5 3.9 copy-start.1
Sparse Core Ops, SparseCore 0:
  9.0 65.4 all-gather.1

commit v2 on v1

--- a/solution.py
+++ b/solution.py
@@ -91,16 +91,23 @@
 
 def gather_kv(block):
     count = lax.axis_size("kv")
+    spread = jnp.broadcast_to(block[None], (count,) + block.shape)
+    return lax.all_to_all(spread, "kv", 0, 0, tiled=True)
+
+
+def reduce_kv(stacked):
+    parts = lax.all_to_all(stacked, "kv", 0, 0, tiled=True)
+    return jnp.sum(parts.astype(jnp.float32), axis=0)
+
+
+def split_columns(block, count):
     rows, width = block.shape
-    spread = jnp.broadcast_to(block[:, None, :], (rows, count, width))
-    return lax.all_to_all(spread, "kv", 1, 1, tiled=True).reshape(rows, count * width)
-
-
-def reduce_kv(block):
-    count = lax.axis_size("kv")
-    rows, width = block.shape
-    parts = lax.all_to_all(block.reshape(rows, count, width // count), "kv", 1, 1, tiled=True)
-    return jnp.sum(parts.astype(jnp.float32), axis=1)
+    return block.reshape(rows, count, width // count).transpose(1, 0, 2)
+
+
+def join_columns(stacked):
+    count, rows, width = stacked.shape
+    return stacked.transpose(1, 0, 2).reshape(rows, count * width)
 
 
 def local(
@@ -124,7 +131,8 @@
     tok_rows = hidden.shape[0]
     slice_width = hidden.shape[1]
     kv_rank = lax.axis_index("kv")
-    full_rows = gather_kv(hidden)
+    kv_count = lax.axis_size("kv")
+    full_rows = join_columns(gather_kv(hidden))
     states = full_rows.astype(jnp.float32)
     normed = rms_scale(states, gain_attn).astype(jnp.bfloat16)
     pool_all = lax.all_gather(kv_pool, "blk", axis=0, tiled=True)
@@ -132,7 +140,7 @@
     page_rows = page_rows.reshape(page_rows.shape[0] * page_rows.shape[1], -1)
     attended = attend(normed, lengths[0], page_rows, w_q, w_k, w_v, sinks)
     partial_value = jnp.dot(attended, w_o, preferred_element_type=jnp.float32)
-    shared = reduce_kv(partial_value.astype(jnp.bfloat16))
+    shared = reduce_kv(split_columns(partial_value.astype(jnp.bfloat16), kv_count))
     residual_slice = hidden.astype(jnp.float32) + shared
     total_sq = lax.psum(jnp.sum(residual_slice * residual_slice, axis=1), "kv")
     gain_slice = lax.dynamic_slice_in_dim(gain_moe, kv_rank * slice_width, slice_width, 0)
@@ -159,17 +167,21 @@
         jnp.bfloat16
     )
     outgoing = outgoing.reshape(blk_count, EXP_DEV * capacity, slice_width)
+    weights, outgoing = lax.optimization_barrier((weights, outgoing))
     items = lax.all_to_all(outgoing, "blk", 0, 0, tiled=True)
-    items = gather_kv(items.reshape(blk_count * EXP_DEV * capacity, slice_width))
-    items = items.reshape(blk_count, EXP_DEV, capacity, -1)
-    gate_val = jnp.einsum("becd,edf->becf", items, w_gate, preferred_element_type=jnp.float32)
-    up_val = jnp.einsum("becd,edf->becf", items, w_up, preferred_element_type=jnp.float32)
+    items = items.reshape(blk_count, EXP_DEV, capacity, slice_width).transpose(1, 0, 2, 3)
+    items = items.reshape(EXP_DEV * blk_count * capacity, slice_width)
+    items = join_columns(gather_kv(items)).reshape(EXP_DEV, blk_count * capacity, -1)
+    gate_val = jnp.einsum("erd,edf->erf", items, w_gate, preferred_element_type=jnp.float32)
+    up_val = jnp.einsum("erd,edf->erf", items, w_up, preferred_element_type=jnp.float32)
     act = swiglu(gate_val, up_val).astype(jnp.bfloat16)
     expert_part = jnp.einsum(
-        "becf,efd->becd", act, w_down, preferred_element_type=jnp.float32
+        "erf,efd->erd", act, w_down, preferred_element_type=jnp.float32
     ).astype(jnp.bfloat16)
-    expert_out = reduce_kv(expert_part.reshape(blk_count * EXP_DEV * capacity, -1))
-    expert_out = expert_out.astype(jnp.bfloat16).reshape(blk_count, EXP_DEV * capacity, slice_width)
+    expert_part = expert_part.reshape(EXP_DEV * blk_count * capacity, -1)
+    expert_out = reduce_kv(split_columns(expert_part, kv_count)).astype(jnp.bfloat16)
+    expert_out = expert_out.reshape(EXP_DEV, blk_count, capacity, slice_width).transpose(1, 0, 2, 3)
+    expert_out = expert_out.reshape(blk_count, EXP_DEV * capacity, slice_width)
     arrived = lax.all_to_all(expert_out, "blk", 0, 0, tiled=True)
     arrived = arrived.reshape(experts * capacity, slice_width)
     picked = jnp.einsum(

time: 591 us -> 606 us (1.025)
  blocking collectives: 301 us -> 314 us
  local copies, waits for them, and re-layouts: 102 us -> 111 us
    convert_element_type x1, local copies, waits for them, and re-layouts: 7.71 us -> 40.3 us  [local(): expert_part = jnp.einsum('erf,efd->erd', act, w_down, preferred_element_t...]
    all_to_all x2 -> x3, blocking collectives: 211 us -> 232 us  [the longest x1 106 us: reduce_kv(): parts = lax.all_to_all(stacked, 'kv', 0, 0, tiled=True)]
    all_to_all x1 -> x0, local copies, waits for them, and re-layouts: 12.7 us -> none  [gather_kv(): lax.all_to_all(spread, 'kv', 1, 1, tiled=True).reshape(rows, count * width)]
    another operation x5 -> x4, local copies, waits for them, and re-layouts: 48.7 us -> 38.2 us  [the longest x1 19.6 us: split_columns(): return block.reshape(rows, count, width // count).transpose(1, 0, 2)]
    psum x1, blocking collectives: 46.8 us -> 38.9 us  [local(): lax.psum(jnp.dot(moe_slice_in, router_rows, preferred_element_type=jnp.fl...]
    all_to_all x3 -> x2, starting transfers between devices: 19.1 us -> 14.7 us  [the longest x1 7.67 us: reduce_kv(): parts = lax.all_to_all(stacked, 'kv', 0, 0, tiled=True)]
    another operation x5 -> x6, other arithmetic: 10.7 us -> 12.6 us
    all_to_all x3 -> x2, waiting for transfers between devices: 33.3 us -> 32.5 us  [the longest x1 23.3 us: gather_kv(): return lax.all_to_all(spread, 'kv', 0, 0, tiled=True)]
  transfers between devices with their start and end apart: 4 -> 3, of which waited for: 3 -> 3; matrix products, arithmetic and copies ran while one was open for 8% -> 6% of each run, Pallas kernels for 0% -> 0%
where the time goes in v2:
time: 606 us; the launch traced here: 594 us
  blocking collectives  314 us (52%)
  local copies, waits for them, and re-layouts  111 us (18%)
  matrix products  51 us (8%)
  waiting for transfers between devices  46.1 us (8%)
  other arithmetic  42.4 us (7%)
  starting transfers between devices  14.7 us (2%)
  between operations  14.7 us (2%)
    all_to_all x1, blocking collectives, reduce_kv(): parts = lax.all_to_all(stacked, 'kv', 0, 0, tiled=True)  106 us
    all_to_all x1, blocking collectives, gather_kv(): return lax.all_to_all(spread, 'kv', 0, 0, tiled=True)  105 us
    convert_element_type x1, local copies, waits for them, and re-layouts, local(): expert_part = jnp.einsum('erf,efd->erd', act, w_down, preferred_element_t...  40.3 us
    psum x1, blocking collectives, local(): lax.psum(jnp.dot(moe_slice_in, router_rows, preferred_element_type=jnp.fl...  38.9 us
    all_to_all x1, waiting for transfers between devices, gather_kv(): return lax.all_to_all(spread, 'kv', 0, 0, tiled=True)  23.3 us
    all_to_all x1, blocking collectives, local(): items = lax.all_to_all(outgoing, 'blk', 0, 0, tiled=True)  23.2 us
    all_to_all x1, blocking collectives, local(): arrived = lax.all_to_all(expert_out, 'blk', 0, 0, tiled=True)  20.7 us
    psum x1, blocking collectives, local(): total_sq = lax.psum(jnp.sum(residual_slice * residual_slice, axis=1), 'kv')  20.5 us
  transfers between devices with their start and end apart: 3, of which 3 were waited for; matrix products, arithmetic and copies ran while one was open for 6% of the time, Pallas kernels for 0%

profile of v2, /device:TPU:0, one launch (start us, length us, event | category | flops | bytes accessed | tf_op | source)
XLA Modules:
  0.0 594.1 jit_solution(4888593005854685905)
XLA Ops:
  9.5 7.0 %all-to-all-start = ((bf16[8,256,360]{1,2,0:T(8,128)(2,1)}), bf16[8,256,360]{1,2,0:T(8,128)(2,1)}, u32[]{:S(2)}, u32[]{:S(2)}) async-start(bf16[8,256,360]{1,2,0:T(8,128)(2,1)} %broadcast_in_dim.84), calls=%async_computation | async-start | bytes 2949120 | tf_op jit(solution)/shard_map/all_to_all | solution.py:95
  19.2 4.6 copy.111
  28.6 23.3 %all-to-all-done = bf16[8,256,360]{1,2,0:T(8,128)(2,1)} async-done(((bf16[8,256,360]{1,2,0:T(8,128)(2,1)}), bf16[8,256,360]{1,2,0:T(8,128)(2,1)}, u32[]{:S(2)}, u32[]{:S(2)}) %all-to-all-start) | async-done | bytes 1474592 | tf_op jit(solution)/shard_map/all_to_all | solution.py:95
  61.7 12.8 %all-gather.2.cloned.1.call-done = bf16[256,128,128]{2,1,0:T(8,128)(2,1)} async-done(((bf16[16,128,128]{2,1,0:T(8,128)(2,1)}), bf16[256,128,128]{2,1,0:T(8,128)(2,1)}) %all-gather.2.cloned.1.call-update) | async-done | bytes 8388624 | tf_op jit(solution)/shard_map/all_gather | solution.py:138
  74.5 5.0 gather_fusion
  85.6 10.3 %fusion.1 = (f32[8,256]{1,0:T(8,128)S(1)}, f32[2304,256,8]{1,0,2:T(8,128)}) fusion(pred[256,2304]{0,1:T(8,128)(4,1)S(1)} %fusion.13, bf16[256,8,32]{0,2,1:T(8,128)(2,1)} %get-tuple-element.12, bf16[256,8,32]{0,2,1:T(8,128)(2,1)} %get-tuple-element.11, bf16[256,1,32]{0,2,1:T(8,128)(2,1)} %get-tuple-element.16, bf16[256,1,32]{0,2,1:T(8,128)(2,1)} %get-tuple-element.15, ...), kind=kOutput, calls=%fused_computation.6 | convolution fusion | flops 619542528 | bytes 20029440 | tf_op jit(solution)/shard_map/tgjd,kgd->gjtk/dot_general | solution.py:68
  96.5 10.2 %fusion = f32[8,256]{1,0:T(8,128)S(1)} fusion(f32[2304,256,8]{1,0,2:T(8,128)} %get-tuple-element.20, f32[8,256]{1,0:T(8,128)S(1)} %broadcast_maximum_fusion, pred[256,2304]{0,1:T(8,128)(4,1)S(1)} %fusion.13), kind=kLoop, calls=%fused_computation.5 | loop fusion | flops 18872320 | bytes 19480576 | tf_op jit(solution)/shard_map/reduce_sum | solution.py:75
  107.6 9.4 %fusion.18 = bf16[64,8,256]{2,0,1:T(8,128)(2,1)S(1)} fusion(f32[8,256]{1,0:T(8,128)S(1)} %exponential_add_fusion, f32[8,256]{1,0:T(8,128)S(1)} %broadcast_maximum_fusion, f32[2304,256,8]{1,0,2:T(8,128)} %get-tuple-element.20, pred[256,2304]{0,1:T(8,128)(4,1)S(1)} %fusion.13, bf16[256,1,64]{0,2,1:T(8,128)(2,1)} %fusion.21, ...), kind=kOutput, calls=%fused_computation.30 | convolution fusion | flops 628293632 | bytes 20037632 | tf_op jit(solution)/shard_map/gjtk,kgd->tgjd/dot_general | solution.py:77
  119.0 7.7 %all-to-all-start.1 = ((bf16[8,256,360]{1,2,0:T(8,128)(2,1)}), bf16[8,256,360]{1,2,0:T(8,128)(2,1)S(1)}, u32[]{:S(2)}, u32[]{:S(2)}) async-start(bf16[8,256,360]{1,2,0:T(8,128)(2,1)} %bitcast.138), calls=%async_computation.1 | async-start | bytes 2949120 | tf_op jit(solution)/shard_map/all_to_all | solution.py:99
  127.4 9.0 %reduce-window.6 = s32[32,8,128]{2,1,0:T(8,128)S(1)} reduce-window(s32[32,8,128]{2,1,0:T(8,128)S(1)} %fusion.39, s32[]{:T(128)} %constant.26.clone.1), window={size=1x1x128 pad=0_0x0_0x127_0}, to_apply=%region_9.10 | reduce-window | flops 4161536 | bytes 262148 | tf_op jit(solution)/shard_map/reduce-window
  139.6 9.2 %all-to-all-done.1 = bf16[8,256,360]{1,2,0:T(8,128)(2,1)S(1)} async-done(((bf16[8,256,360]{1,2,0:T(8,128)(2,1)}), bf16[8,256,360]{1,2,0:T(8,128)(2,1)S(1)}, u32[]{:S(2)}, u32[]{:S(2)}) %all-to-all-start.1) | async-done | bytes 1474592 | tf_op jit(solution)/shard_map/all_to_all | solution.py:99
  149.2 20.5 %psum.14 = f32[256]{0:T(256)S(1)} all-reduce(f32[256]{0:T(256)S(1)} %multiply_reduce_fusion.2), channel_id=1, replica_groups=mesh['blk'=16,'kv'=8] {'kv'}, use_global_device_ids=true, to_apply=%region_5.6 | all-reduce | flops 256 | bytes 2048 | tf_op jit(solution)/shard_map/psum | solution.py:145
  170.8 38.9 %psum.15 = f32[256,32]{0,1:T(8,128)S(1)} all-reduce(f32[256,32]{0,1:T(8,128)S(1)} %fusion.48), channel_id=1, replica_groups=mesh['blk'=16,'kv'=8] {'kv'}, use_global_device_ids=true, to_apply=%region_6.7 | all-reduce | flops 8192 | bytes 65536 | tf_op jit(solution)/shard_map/psum | solution.py:153
  209.6 8.6 %gather_fusion.1 = f32[1024]{0:T(1024)S(1)} fusion(f32[256,32]{0,1:T(8,128)S(1)} %psum.15, s32[1024]{0:T(1024)S(1)} %reshape.446), kind=kCustom, calls=%fused_computation.1 | custom fusion | bytes 16384 | tf_op jit(solution)/shard_map/jit(take_along_axis)/gather | solution.py:156
  219.8 23.2 %all_to_all.30 = bf16[16,96,360]{2,1,0:T(8,128)(2,1)S(1)} all-to-all(bf16[16,96,360]{2,1,0:T(8,128)(2,1)S(1)} %bitcast.132), channel_id=1, replica_groups=mesh['blk'=16,'kv'=8] {'blk'}, dimensions={0} | all-to-all | bytes 2211840 | tf_op jit(solution)/shard_map/all_to_all | solution.py:171
  244.4 104.8 %all_to_all.31 = bf16[8,1536,360]{1,2,0:T(8,128)(2,1)} all-to-all(bf16[8,1536,360]{1,2,0:T(8,128)(2,1)S(1)} %broadcast_in_dim.91), channel_id=1, replica_groups=mesh['blk'=16,'kv'=8] {'kv'}, dimensions={0} | all-to-all | bytes 17694720 | tf_op jit(solution)/shard_map/all_to_all | solution.py:95
  349.2 18.5 %reshape_reshape.7 = bf16[2,768,2880]{1,0,2:T(2,128)(2,1)} reshape(bf16[1536,8,360]{0,2,1:T(8,128)(2,1)} %bitcast.130) | data formatting | bytes 17694720 | tf_op jit(solution)/shard_map/reshape;reshape | solution.py:174
  367.7 8.3 %fusion.6 = f32[2,768,360]{1,2,0:T(8,128)S(1)} fusion(bf16[2,2880,360]{1,2,0:T(8,128)(2,1)} %param.26, bf16[2,768,2880]{1,0,2:T(2,128)(2,1)} %reshape_reshape.7), kind=kOutput, calls=%fused_computation.11 | convolution fusion | flops 3185049600 | bytes 15206400 | tf_op jit(solution)/shard_map/erd,edf->erf/dot_general | solution.py:176
  376.0 15.5 %convolution_convert_fusion = bf16[2,768,2880]{1,2,0:T(8,128)(2,1)} fusion(bf16[2,360,2880]{2,1,0:T(8,128)(2,1)} %param.27, f32[2,768,360]{1,2,0:T(8,128)S(1)} %fusion.6, bf16[2,2880,360]{1,2,0:T(8,128)(2,1)} %param.25, bf16[2,768,2880]{1,0,2:T(2,128)(2,1)} %reshape_reshape.7), kind=kOutput, calls=%fused_computation.13 | convolution fusion | flops 6380052480 | bytes 28200960 | tf_op jit(solution)/shard_map/erf,efd->erd/dot_general | solution.py:178
  391.5 40.3 %copy.125 = bf16[2,768,2880]{1,0,2:T(2,128)(2,1)} copy(bf16[2,768,2880]{1,2,0:T(8,128)(2,1)} %convolution_convert_fusion) | data formatting | bytes 17694720 | tf_op jit(solution)/shard_map/convert_element_type | solution.py:180
  431.8 19.6 %reshape_reshape.8 = bf16[1536,8,360]{0,2,1:T(8,128)(2,1)} reshape(bf16[2,768,2880]{1,0,2:T(2,128)(2,1)} %copy.125) | data formatting | bytes 17694720 | tf_op jit(solution)/shard_map/reshape;reshape | solution.py:105
  451.4 106.3 %all_to_all.32 = bf16[8,1536,360]{1,2,0:T(8,128)(2,1)} all-to-all(bf16[8,1536,360]{1,2,0:T(8,128)(2,1)} %bitcast.131), channel_id=1, replica_groups=mesh['blk'=16,'kv'=8] {'kv'}, dimensions={0} | all-to-all | bytes 17694720 | tf_op jit(solution)/shard_map/all_to_all | solution.py:99
  557.7 5.4 reduce_sum.75
  564.0 20.7 %all_to_all.33 = bf16[16,96,360]{2,1,0:T(8,128)(2,1)S(1)} all-to-all(bf16[16,96,360]{2,1,0:T(8,128)(2,1)S(1)} %bitcast.136), channel_id=1, replica_groups=mesh['blk'=16,'kv'=8] {'blk'}, dimensions={0} | all-to-all | bytes 2211840 | tf_op jit(solution)/shard_map/all_to_all | solution.py:185
  (108 shorter events, 40.3 us)
Async XLA Ops:
  6.5 110.4 %copy-start = (bf16[512,2880]{0,1:T(8,128)(2,1)S(1)}, bf16[512,2880]{0,1:T(8,128)(2,1)}, u32[]{:S(2)}) copy-start(bf16[512,2880]{0,1:T(8,128)(2,1)} %param.22) | copy-start | bytes 8847364
  6.5 10.7 %copy-start.19 = (s32[1,16]{1,0:T(1,128)S(1)}, s32[1,16]{1,0:T(1,128)}, u32[]{:S(2)}) copy-start(s32[1,16]{1,0:T(1,128)} %param.29) | copy-start | bytes 196
  6.5 11.9 %copy-start.10 = (f32[2880]{0:T(1024)S(1)}, f32[2880]{0:T(1024)}, u32[]{:S(2)}) copy-start(f32[2880]{0:T(1024)} %param.17) | copy-start | bytes 34564
  6.5 68.0 %all-gather.2.cloned.1.call-start = ((), (), s32[]{:S(2)}) async-start(), calls=%async_computation.6 | async-start | bytes 8912896 | tf_op jit(solution)/shard_map/all_gather | solution.py:138
  9.5 42.4 %all-to-all-start = ((bf16[8,256,360]{1,2,0:T(8,128)(2,1)}), bf16[8,256,360]{1,2,0:T(8,128)(2,1)}, u32[]{:S(2)}, u32[]{:S(2)}) async-start(bf16[8,256,360]{1,2,0:T(8,128)(2,1)} %broadcast_in_dim.84), calls=%async_computation | async-start | bytes 2949120 | tf_op jit(solution)/shard_map/all_to_all | solution.py:95
  17.2 7.2 %copy-start.14 = (f32[256]{0:T(256)}, f32[256]{0:T(256)S(1)}, u32[]{:S(2)}) copy-start(f32[256]{0:T(256)S(1)} %add_convert_fusion.2) | copy-start | bytes 3076
  18.5 6.0 %copy-start.16 = (f32[32]{0:T(128)}, f32[32]{0:T(128)S(1)}, u32[]{:S(2)}) copy-start(f32[32]{0:T(128)S(1)} %multiply_power_fusion) | copy-start | bytes 388
  51.9 3.8 copy-start.5
  51.9 4.8 copy-start.6
  53.8 3.3 copy-start.15
  53.8 3.3 copy-start.17
  53.8 4.1 copy-start.11
  56.7 3.2 copy-start.2
  59.8 1.0 copy-start.7
  59.8 1.0 copy-start.8
  60.9 22.9 %copy-start.13 = (pred[2048]{0:T(1024)(128)(4,1)S(1)}, pred[2048]{0:T(1024)(128)(4,1)}, u32[]{:S(2)}) copy-start(pred[2048]{0:T(1024)(128)(4,1)} %broadcast_bitcast_fusion) | copy-start | bytes 6148
  85.6 10.3 %copy-start.18 = (f32[8]{0:T(128)S(1)}, f32[8]{0:T(128)}, u32[]{:S(2)}) copy-start(f32[8]{0:T(128)} %param.21) | copy-start | bytes 100
  95.9 0.6 copy-start.12
  119.0 7.7 %copy-start.9 = (s32[256,4]{0,1:T(4,128)S(1)}, s32[256,4]{0,1:T(4,128)}, u32[]{:S(2)}) copy-start(s32[256,4]{0,1:T(4,128)} %param.31) | copy-start | bytes 12292
  119.0 29.9 %all-to-all-start.1 = ((bf16[8,256,360]{1,2,0:T(8,128)(2,1)}), bf16[8,256,360]{1,2,0:T(8,128)(2,1)S(1)}, u32[]{:S(2)}, u32[]{:S(2)}) async-start(bf16[8,256,360]{1,2,0:T(8,128)(2,1)} %bitcast.138), calls=%async_computation.1 | async-start | bytes 2949120 | tf_op jit(solution)/shard_map/all_to_all | solution.py:99
  126.7 22.4 %copy-start.3 = (bf16[256,360]{0,1:T(8,128)(2,1)S(1)}, bf16[256,360]{0,1:T(8,128)(2,1)}, u32[]{:S(2)}) copy-start(bf16[256,360]{0,1:T(8,128)(2,1)} %param.16) | copy-start | bytes 552964
  209.6 8.9 %copy-start.4 = (pred[256,1536]{1,0:T(8,128)(4,1)S(1)}, pred[256,1536]{1,0:T(8,128)(4,1)}, u32[]{:S(2)}) copy-start(pred[256,1536]{1,0:T(8,128)(4,1)} %fusion.9) | copy-start | bytes 1179652
  584.6 2.5 copy-start.1
Sparse Core Ops, SparseCore 0:
  9.0 65.4 all-gather.1
